TPU v7x, 128 devices: a whole 4x4x4 slice. The times are simulated.
128 devices in a mesh: seq: 16 (over z, x), hid: 4 (over y), rep: 2 (over core).
Axes of the slice: x: 4, y: 4, z: 4, core: 2. Of those that a mesh axis runs over, the one named last changes fastest.
Arguments:
- tokens: bfloat16 [16384, 5376], P(('rep', 'seq'), 'hid'), parts along dimension 0, may hold values from -6 to 6
- norm_gain: float32 [5376], replicated, may hold values from 0.1 to 1.9
- w_query: bfloat16 [5376, 4096], P('seq', 'hid'), may hold values from -0.078125 to 0.078125
- w_key: bfloat16 [5376, 2048], P('seq', 'hid'), may hold values from -0.078125 to 0.078125
- w_value: bfloat16 [5376, 2048], P('seq', 'hid'), may hold values from -0.078125 to 0.078125
- query_gain: float32 [128], replicated, may hold values from 0.5 to 8
- key_gain: float32 [128], replicated, may hold values from 0.5 to 8
- w_out: bfloat16 [4096, 5376], P('hid', 'seq'), may hold values from -0.09375 to 0.09375
Outputs:
- attended: bfloat16 [16384, 5376], P(('rep', 'seq'), 'hid'), parts along dimension 0
There are 2 independent parts, one for each index of `rep`. A program takes and returns all parts, laid end to end along the dimension named above; an argument that names none is the same for every part. Nothing has to cross between parts.
All inputs are finite; a program needn't handle non-finite values.
Results may differ from a plain program's by a relative error of at most 0.023.
The roundings to bfloat16 on the way count: a program that leaves them out, or rounds other values in their place, can miss the bound.
Values may be sent and summed in bfloat16 or wider, within the bound.
A program may use at most 128 MiB of HBM per device.

v0:
```python
import jax
import jax.numpy as jnp
from jax import lax
from jax.sharding import PartitionSpec as P

HEAD_WIDTH = 128
WINDOW = 1024
QSCALE = 168
DEPTH = 2


def shifted(x, axis, by):
    count = lax.axis_size(axis)
    pairs = [(i, i + by) for i in range(count) if 0 <= i + by < count]
    return lax.ppermute(x, axis, pairs)


def rope(heads, positions):
    half = heads.shape[-1] // 2
    freq = 10000.0 ** (-(jnp.arange(half, dtype=jnp.float32) * 2.0) / heads.shape[-1])
    angle = positions[:, None] * freq[None, :]
    cosine = jnp.cos(angle)[:, None, :]
    sine = jnp.sin(angle)[:, None, :]
    first = heads[..., :half]
    second = heads[..., half:]
    return jnp.concatenate(
        [first * cosine - second * sine, second * cosine + first * sine], axis=-1
    )


def head_norm(heads, gain):
    return heads * lax.rsqrt(jnp.mean(heads * heads, axis=-1, keepdims=True) + 1e-06) * gain


def add_rows(normed, piece):
    return jnp.dot(normed, piece, preferred_element_type=jnp.float32)


def shards(tokens, norm_gain, w_query, w_key, w_value, query_gain, key_gain, w_out):
    whole = lax.all_gather(tokens, "hid", axis=1, tiled=True)
    xfloat = whole.astype(jnp.float32)
    normed = (
        xfloat * lax.rsqrt(jnp.mean(xfloat * xfloat, axis=-1, keepdims=True) + 1e-06) * norm_gain
    ).astype(jnp.bfloat16)
    rows = normed.shape[0]

    def add_one(piece):
        return add_rows(normed, piece)

    query = add_one(lax.all_gather(w_query, "seq", axis=0, tiled=True))
    key = add_one(lax.all_gather(w_key, "seq", axis=0, tiled=True))
    value = add_one(lax.all_gather(w_value, "seq", axis=0, tiled=True))
    local_heads = w_query.shape[1] // HEAD_WIDTH
    local_kv = w_key.shape[1] // HEAD_WIDTH
    base = lax.axis_index("seq") * rows
    qpos = base + jnp.arange(rows, dtype=jnp.int32)
    positions = qpos.astype(jnp.float32)
    qh = (
        rope(head_norm(query.reshape(rows, local_heads, HEAD_WIDTH), query_gain), positions)
        * QSCALE ** (-0.5)
    ).astype(jnp.bfloat16)
    kh = rope(head_norm(key.reshape(rows, local_kv, HEAD_WIDTH), key_gain), positions).astype(
        jnp.bfloat16
    )
    value_head = value.reshape(rows, local_kv, HEAD_WIDTH).astype(jnp.bfloat16)
    key_blocks = []
    value_blocks = []
    for distance in range(1, DEPTH + 1):
        arrived = shifted((kh, value_head), "seq", distance)
        key_blocks.insert(0, arrived[0])
        value_blocks.insert(0, arrived[1])
    keys = jnp.concatenate(key_blocks + [kh], axis=0)
    values = jnp.concatenate(value_blocks + [value_head], axis=0)
    window_extent = keys.shape[0]
    kpos = base - DEPTH * rows + jnp.arange(window_extent, dtype=jnp.int32)
    diff = qpos[:, None] - kpos[None, :]
    allowed = (diff >= 0) & (diff < WINDOW) & (kpos >= 0)[None, :]
    group = local_heads // local_kv
    grouped = qh.reshape(rows, local_kv, group, HEAD_WIDTH).transpose(1, 0, 2, 3)

    def one_head(operands):
        qpart, kpart, vpart = operands
        scores = jnp.einsum("rgd,ld->grl", qpart, kpart, preferred_element_type=jnp.float32)
        scores = jnp.where(allowed[None], scores, -jnp.inf)
        probs = jax.nn.softmax(scores, axis=-1).astype(jnp.bfloat16)
        mixed = jnp.einsum("grl,ld->rgd", probs, vpart, preferred_element_type=jnp.float32)
        return mixed.astype(jnp.bfloat16)

    per_head = lax.map(one_head, (grouped, keys.transpose(1, 0, 2), values.transpose(1, 0, 2)))
    heads_out = per_head.transpose(1, 0, 2, 3).reshape(rows, local_heads * HEAD_WIDTH)
    terms = jnp.dot(
        heads_out,
        lax.all_gather(w_out, "seq", axis=1, tiled=True),
        preferred_element_type=jnp.float32,
    )
    return lax.psum_scatter(terms.astype(jnp.bfloat16), "hid", scatter_dimension=1, tiled=True)


def solution(mesh):
    return jax.shard_map(
        shards,
        mesh=mesh,
        in_specs=(
            P(("rep", "seq"), "hid"),
            P(),
            P("seq", "hid"),
            P("seq", "hid"),
            P("seq", "hid"),
            P(),
            P(),
            P("hid", "seq"),
        ),
        out_specs=P(("rep", "seq"), "hid"),
        check_vma=False,
    )
```

profile of v0, /device:TPU:1, one launch (start us, length us, event | category | flops | bytes accessed | tf_op | source)
XLA Modules:
  0.0 466.9 jit_solution(10605443407271170900)
XLA Ops:
  11.0 60.4 %all-gather.6.cloned.1.call-done = bf16[512,5376]{0,1:T(8,128)(2,1)} async-done(((bf16[512,1344]{0,1:T(8,128)(2,1)}), bf16[512,5376]{0,1:T(8,128)(2,1)}) %all-gather.6.cloned.1.call-update) | async-done | bytes 5505040 | tf_op jit(solution)/shard_map/all_gather | solution.py:40
  71.4 3.8 fusion.41
  75.2 56.7 %all-gather.10.cloned.1.call-done = bf16[5376,512]{1,0:T(8,128)(2,1)} async-done(((bf16[336,512]{1,0:T(8,128)(2,1)}), bf16[5376,512]{1,0:T(8,128)(2,1)}) %all-gather.10.cloned.1.call-update) | async-done | bytes 5505040 | tf_op jit(solution)/shard_map/all_gather | solution.py:51
  131.9 7.6 %multiply_reduce_fusion.1 = (f32[512,4]{0,1:T(4,128)S(1)}, f32[512,512]{0,1:T(8,128)S(1)}) fusion(bf16[5376,512]{1,0:T(8,128)(2,1)} %all-gather.10.cloned.1.call-done, bf16[512,5376]{0,1:T(8,128)(2,1)} %all-gather.6.cloned.1.call-done, f32[5376]{0:T(1024)S(1)} %copy-done.2, f32[512]{0:T(512)S(1)} %add_rsqrt_fusion.2), kind=kOutput, calls=%fused_computation.52 | convolution fusion | flops 2830104576 | bytes 12090368 | tf_op jit(solution)/shard_map/dot_general | solution.py:36
  141.0 4.6 collective-permute-start.2
  145.6 2.2 collective-permute-start.3
  147.9 54.8 %all-gather.8.cloned.1.call-done = bf16[5376,512]{1,0:T(8,128)(2,1)} async-done(((bf16[336,512]{1,0:T(8,128)(2,1)}), bf16[5376,512]{1,0:T(8,128)(2,1)}) %all-gather.8.cloned.1.call-update) | async-done | bytes 5505040 | tf_op jit(solution)/shard_map/all_gather | solution.py:52
  202.7 8.4 %convolution_convert_fusion.1 = bf16[512,512]{0,1:T(8,128)(2,1)} fusion(bf16[5376,512]{1,0:T(8,128)(2,1)} %all-gather.8.cloned.1.call-done, bf16[512,5376]{0,1:T(8,128)(2,1)} %all-gather.6.cloned.1.call-done, f32[5376]{0:T(1024)S(1)} %copy-done.2, f32[512]{0:T(512)S(1)} %add_rsqrt_fusion.2), kind=kOutput, calls=%fused_computation.47 | convolution fusion | flops 2829844480 | bytes 11557888 | tf_op jit(solution)/shard_map/dot_general | solution.py:36
  211.1 5.4 %collective-permute-start = (bf16[512,4,128]{0,2,1:T(8,128)(2,1)}, bf16[512,4,128]{0,2,1:T(8,128)(2,1)}, u32[]{:S(2)}, u32[]{:S(2)}) collective-permute-start(bf16[512,4,128]{0,2,1:T(8,128)(2,1)} %bitcast), channel_id=1, source_target_pairs={{0,16},{8,24},{16,32},{24,40},{32,48},{40,56},{48,64},{56,72},{64,... | collective-permute-start | bytes 1572872 | tf_op jit(solution)/shard_map/ppermute | solution.py:15
  216.5 3.0 collective-permute-start.1
  219.6 1.5 maximum_bitcast_fusion.1
  221.1 12.3 %collective-permute-done = bf16[512,4,128]{0,2,1:T(8,128)(2,1)} collective-permute-done((bf16[512,4,128]{0,2,1:T(8,128)(2,1)}, bf16[512,4,128]{0,2,1:T(8,128)(2,1)}, u32[]{:S(2)}, u32[]{:S(2)}) %collective-permute-start) | collective-permute-done | bytes 524320 | tf_op jit(solution)/shard_map/ppermute | solution.py:15
  233.4 15.0 %collective-permute-done.1 = bf16[512,4,128]{0,2,1:T(8,128)(2,1)} collective-permute-done((bf16[512,4,128]{0,2,1:T(8,128)(2,1)}, bf16[512,4,128]{0,2,1:T(8,128)(2,1)}, u32[]{:S(2)}, u32[]{:S(2)}) %collective-permute-start.1) | collective-permute-done | bytes 524320 | tf_op jit(solution)/shard_map/ppermute | solution.py:15
  248.5 2.6 maximum_bitcast_fusion
  251.0 55.3 %all-gather.12.cloned.1.call-done = bf16[5376,1024]{1,0:T(8,128)(2,1)} async-done(((bf16[336,1024]{1,0:T(8,128)(2,1)}), bf16[5376,1024]{1,0:T(8,128)(2,1)}) %all-gather.12.cloned.1.call-update) | async-done | bytes 11010064 | tf_op jit(solution)/shard_map/all_gather | solution.py:50
  306.4 11.7 %convolution_bitcast_fusion = f32[64,8,8,128]{3,1,2,0:T(8,128)S(1)} fusion(bf16[5376,1024]{1,0:T(8,128)(2,1)} %all-gather.12.cloned.1.call-done, bf16[512,5376]{0,1:T(8,128)(2,1)} %all-gather.6.cloned.1.call-done, f32[5376]{0:T(1024)S(1)} %copy-done.2, f32[512]{0:T(512)S(1)} %add_rsqrt_fusion.2), kind=kOutput, calls=%fused_computation.44 | convolution fusion | flops 5648154624 | bytes 18635776 | tf_op jit(solution)/shard_map/dot_general | solution.py:36
  323.6 43.2 %while.11 = (s32[]{:T(128)}, bf16[4,512,2,128]{1,3,2,0:T(8,128)(2,1)S(1)}, bf16[4,1536,128]{1,2,0:T(8,128)(2,1)}, bf16[4,1536,128]{2,1,0:T(8,128)(2,1)}, bf16[4,...) while((s32[]{:T(128)}, ...), condition=%wide.region_6.7_spmd.clone, body=%wide.region_3.6_spmd.clone.sunk | while | flops 817235456 | bytes 15486557 | solution.py:89
  323.6 1.2 fusion.74
  324.8 5.8 %fusion.75 = (f32[2,512]{1,0:T(2,128)S(1)}, f32[2,512,1536]{1,2,0:T(8,128)}) fusion(pred[512,1536]{0,1:T(8,128)(4,1)S(1)} %fusion.74, bf16[4,1536,128]{2,1,0:T(8,128)(2,1)} %get-tuple-element.159, s32[]{:T(128)} %get-tuple-element.147, bf16[4,512,2,128]{3,1,2,0:T(8,128)(2,1)S(1)} %get-tuple-element.160), kind=kOutput, calls=%fused_computation.65.clone.1 | convolution fusion | flops 407373312 | bytes 7738368 | tf_op jit(solution)/shard_map/while/body/eval_jaxpr/sub | solution.py:85
  330.6 3.6 fusion.76
  334.2 1.2 fusion.74
  335.4 5.8 %fusion.75 = (f32[2,512]{1,0:T(2,128)S(1)}, f32[2,512,1536]{1,2,0:T(8,128)}) fusion(pred[512,1536]{0,1:T(8,128)(4,1)S(1)} %fusion.74, bf16[4,1536,128]{2,1,0:T(8,128)(2,1)} %get-tuple-element.159, s32[]{:T(128)} %get-tuple-element.147, bf16[4,512,2,128]{3,1,2,0:T(8,128)(2,1)S(1)} %get-tuple-element.160), kind=kOutput, calls=%fused_computation.65.clone.1 | convolution fusion | flops 407373312 | bytes 7738368 | tf_op jit(solution)/shard_map/while/body/eval_jaxpr/sub | solution.py:85
  341.2 4.3 fusion.76
  345.6 1.2 fusion.74
  346.8 5.8 %fusion.75 = (f32[2,512]{1,0:T(2,128)S(1)}, f32[2,512,1536]{1,2,0:T(8,128)}) fusion(pred[512,1536]{0,1:T(8,128)(4,1)S(1)} %fusion.74, bf16[4,1536,128]{2,1,0:T(8,128)(2,1)} %get-tuple-element.159, s32[]{:T(128)} %get-tuple-element.147, bf16[4,512,2,128]{3,1,2,0:T(8,128)(2,1)S(1)} %get-tuple-element.160), kind=kOutput, calls=%fused_computation.65.clone.1 | convolution fusion | flops 407373312 | bytes 7738368 | tf_op jit(solution)/shard_map/while/body/eval_jaxpr/sub | solution.py:85
  352.6 3.6 fusion.76
  356.2 1.2 fusion.74
  357.4 5.8 %fusion.75 = (f32[2,512]{1,0:T(2,128)S(1)}, f32[2,512,1536]{1,2,0:T(8,128)}) fusion(pred[512,1536]{0,1:T(8,128)(4,1)S(1)} %fusion.74, bf16[4,1536,128]{2,1,0:T(8,128)(2,1)} %get-tuple-element.159, s32[]{:T(128)} %get-tuple-element.147, bf16[4,512,2,128]{3,1,2,0:T(8,128)(2,1)S(1)} %get-tuple-element.160), kind=kOutput, calls=%fused_computation.65.clone.1 | convolution fusion | flops 407373312 | bytes 7738368 | tf_op jit(solution)/shard_map/while/body/eval_jaxpr/sub | solution.py:85
  363.2 3.5 fusion.76
  366.8 24.1 %all-gather.14.cloned.1.call-done = bf16[1024,5376]{0,1:T(8,128)(2,1)} async-done(((bf16[1024,336]{0,1:T(8,128)(2,1)}), bf16[1024,5376]{0,1:T(8,128)(2,1)}) %all-gather.14.cloned.1.call-update) | async-done | bytes 11010064 | tf_op jit(solution)/shard_map/all_gather | solution.py:93
  390.9 11.8 %convolution_convert_fusion = bf16[512,5376]{0,1:T(8,128)(2,1)} fusion(bf16[1024,5376]{0,1:T(8,128)(2,1)} %all-gather.14.cloned.1.call-done, bf16[512,1024]{0,1:T(8,128)(2,1)S(1)} %bitcast.83), kind=kOutput, calls=%fused_computation.37 | convolution fusion | flops 5639897088 | bytes 17563648 | tf_op jit(solution)/shard_map/dot_general | solution.py:91
  402.7 57.3 %reduce-scatter.2.cloned.1.call-done = bf16[512,1344]{0,1:T(8,128)(2,1)} async-done(((bf16[512,5376]{0,1:T(8,128)(2,1)}), bf16[512,1344]{0,1:T(8,128)(2,1)}) %reduce-scatter.2.cloned.1.call-update) | async-done | bytes 1376272 | tf_op jit(solution)/shard_map/reduce_scatter | solution.py:96
  (45 shorter events, 11.2 us)
Async XLA Ops:
  6.5 64.9 %all-gather.6.cloned.1.call-start = ((), (), s32[]{:S(2)}) async-start(), calls=%async_computation.1 | async-start | bytes 6881280 | tf_op jit(solution)/shard_map/all_gather | solution.py:40
  7.3 124.7 %all-gather.10.cloned.1.call-start = ((), (), s32[]{:S(2)}) async-start(), calls=%async_computation.3 | async-start | bytes 5849088 | tf_op jit(solution)/shard_map/all_gather | solution.py:51
  8.0 194.7 %all-gather.8.cloned.1.call-start = ((), (), s32[]{:S(2)}) async-start(), calls=%async_computation.2 | async-start | bytes 5849088 | tf_op jit(solution)/shard_map/all_gather | solution.py:52
  8.7 297.6 %all-gather.12.cloned.1.call-start = ((), (), s32[]{:S(2)}) async-start(), calls=%async_computation.4 | async-start | bytes 11698176 | tf_op jit(solution)/shard_map/all_gather | solution.py:50
  9.3 381.6 %all-gather.14.cloned.1.call-start = ((), (), s32[]{:S(2)}) async-start(), calls=%async_computation.5 | async-start | bytes 11698176 | tf_op jit(solution)/shard_map/all_gather | solution.py:93
  9.9 122.0 %copy-start.2 = (f32[5376]{0:T(1024)S(1)}, f32[5376]{0:T(1024)}, u32[]{:S(2)}) copy-start(f32[5376]{0:T(1024)} %param.11) | copy-start | bytes 64516
  9.9 450.1 %reduce-scatter.2.cloned.1.call-start = ((), (), s32[]{:S(2)}) async-start(), calls=%async_computation.6 | async-start | bytes 6881280 | tf_op jit(solution)/shard_map/reduce_scatter | solution.py:96
  75.2 64.7 %copy-start = (f32[128]{0:T(128)S(1)}, f32[128]{0:T(128)}, u32[]{:S(2)}) copy-start(f32[128]{0:T(128)} %param.16) | copy-start | bytes 1540
  141.0 78.6 %collective-permute-start.2 = (bf16[512,4,128]{2,0,1:T(8,128)(2,1)S(1)}, bf16[512,4,128]{2,0,1:T(8,128)(2,1)S(1)}, u32[]{:S(2)}, u32[]{:S(2)}) collective-permute-start(bf16[512,4,128]{2,0,1:T(8,128)(2,1)S(1)} %pad_maximum_fusion), channel_id=1, source_target_pairs={{0,16},{8,24},{16,32},{24,40},{32,48},{40,56},{48,64},{56,72},{64,... | collective-permute-start | bytes 1572872 | tf_op jit(solution)/shard_map/ppermute | solution.py:15
  145.6 73.9 %collective-permute-start.3 = (bf16[512,4,128]{2,0,1:T(8,128)(2,1)S(1)}, bf16[512,4,128]{2,0,1:T(8,128)(2,1)S(1)}, u32[]{:S(2)}, u32[]{:S(2)}) collective-permute-start(bf16[512,4,128]{2,0,1:T(8,128)(2,1)S(1)} %pad_maximum_fusion), channel_id=1, source_target_pairs={{0,8},{8,16},{16,24},{24,32},{32,40},{40,48},{48,56},{56,64},{64,7... | collective-permute-start | bytes 1572872 | tf_op jit(solution)/shard_map/ppermute | solution.py:15
  211.1 22.3 %collective-permute-start = (bf16[512,4,128]{0,2,1:T(8,128)(2,1)}, bf16[512,4,128]{0,2,1:T(8,128)(2,1)}, u32[]{:S(2)}, u32[]{:S(2)}) collective-permute-start(bf16[512,4,128]{0,2,1:T(8,128)(2,1)} %bitcast), channel_id=1, source_target_pairs={{0,16},{8,24},{16,32},{24,40},{32,48},{40,56},{48,64},{56,72},{64,... | collective-permute-start | bytes 1572872 | tf_op jit(solution)/shard_map/ppermute | solution.py:15
  216.5 31.9 %collective-permute-start.1 = (bf16[512,4,128]{0,2,1:T(8,128)(2,1)}, bf16[512,4,128]{0,2,1:T(8,128)(2,1)}, u32[]{:S(2)}, u32[]{:S(2)}) collective-permute-start(bf16[512,4,128]{0,2,1:T(8,128)(2,1)} %bitcast), channel_id=1, source_target_pairs={{0,8},{8,16},{16,24},{24,32},{32,40},{40,48},{48,56},{56,64},{64,7... | collective-permute-start | bytes 1572872 | tf_op jit(solution)/shard_map/ppermute | solution.py:15
  318.1 1.4 copy-start.1
  322.3 1.2 copy-start.3
Sparse Core Ops, SparseCore 0:
  9.0 62.3 all-gather.5
  73.5 58.3 all-gather.9
  134.1 68.5 all-gather.7
  204.7 101.6 all-gather.11
  308.3 82.4 all-gather.13
  402.8 57.1 reduce-scatter.1
where the time goes:
time: 467 us
  waiting for transfers between devices  339 us (73%)
  matrix products  77.8 us (17%)
  other arithmetic  18.1 us (4%)
  starting transfers between devices  15.5 us (3%)
  between operations  13.7 us (3%)
    all_gather x1, waiting for transfers between devices, shards(): whole = lax.all_gather(tokens, 'hid', axis=1, tiled=True)  60.4 us
    reduce_scatter x1, waiting for transfers between devices, shards(): lax.psum_scatter(terms.astype(jnp.bfloat16), 'hid', scatter_dimension=1,...  57.3 us
    all_gather x1, waiting for transfers between devices, shards(): key = add_one(lax.all_gather(w_key, 'seq', axis=0, tiled=True))  56.7 us
    all_gather x1, waiting for transfers between devices, shards(): query = add_one(lax.all_gather(w_query, 'seq', axis=0, tiled=True))  55.3 us
    all_gather x1, waiting for transfers between devices, shards(): value = add_one(lax.all_gather(w_value, 'seq', axis=0, tiled=True))  54.8 us
    dot_general x3, matrix products, add_rows(): return jnp.dot(normed, piece, preferred_element_type=jnp.float32)  27.7 us
    ppermute x4, waiting for transfers between devices, shifted(): return lax.ppermute(x, axis, pairs)  27.4 us
    all_gather x1, waiting for transfers between devices, shards(): lax.all_gather(w_out, 'seq', axis=1, tiled=True)  24.1 us
  transfers between devices with their start and end apart: 10, of which 8 were waited for; matrix products, arithmetic and copies ran while one was open for 18% of the time, Pallas kernels for 0%

commit v1 on v0

--- a/solution.py
+++ b/solution.py
@@ -7,6 +7,24 @@
 WINDOW = 1024
 QSCALE = 168
 DEPTH = 2
+
+
+def collect(shard, axis, dim):
+    ways, here, lap = (lax.axis_size(axis), lax.axis_index(axis), shard.shape[dim])
+    shape = [n * ways if d == dim else n for d, n in enumerate(shard.shape)]
+    full = lax.dynamic_update_slice_in_dim(
+        jnp.zeros(shape, shard.dtype), shard, here * lap, axis=dim
+    )
+    going_up = going_down = shard
+    for far in range(1, ways // 2 + 1):
+        going_up = lax.ppermute(going_up, axis, [(d, (d + 1) % ways) for d in range(ways)])
+        full = lax.dynamic_update_slice_in_dim(full, going_up, (here - far) % ways * lap, axis=dim)
+        if 2 * far < ways:
+            going_down = lax.ppermute(going_down, axis, [(d, (d - 1) % ways) for d in range(ways)])
+            full = lax.dynamic_update_slice_in_dim(
+                full, going_down, (here + far) % ways * lap, axis=dim
+            )
+    return full
 
 
 def shifted(x, axis, by):
@@ -49,7 +67,7 @@
 
     query = add_one(lax.all_gather(w_query, "seq", axis=0, tiled=True))
     key = add_one(lax.all_gather(w_key, "seq", axis=0, tiled=True))
-    value = add_one(lax.all_gather(w_value, "seq", axis=0, tiled=True))
+    value = add_one(collect(w_value, "seq", 0))
     local_heads = w_query.shape[1] // HEAD_WIDTH
     local_kv = w_key.shape[1] // HEAD_WIDTH
     base = lax.axis_index("seq") * rows

time: 467 us -> 415 us (0.89)
  waiting for transfers between devices: 339 us -> 235 us
  starting transfers between devices: 15.5 us -> 51.6 us
  local copies, waits for them, and re-layouts: 2.44 us -> 17.1 us
    all_gather x1, waiting for transfers between devices: 60.4 us -> 0.01 us  [shards(): whole = lax.all_gather(tokens, 'hid', axis=1, tiled=True)]
    all_gather x1 -> x0, waiting for transfers between devices: 54.8 us -> none  [shards(): value = add_one(lax.all_gather(w_value, 'seq', axis=0, tiled=True))]
    ppermute x0 -> x15, waiting for transfers between devices: none -> 38.5 us  [the longest x8 28.4 us: collect(): lax.ppermute(going_up, axis, [(d, (d + 1) % ways) for d in range(ways)])]
    ppermute x0 -> x15, starting transfers between devices: none -> 37 us  [the longest x7 34.9 us: collect(): lax.ppermute(going_down, axis, [(d, (d - 1) % ways) for d in range(ways)])]
    all_gather x1, waiting for transfers between devices: 56.7 us -> 33.9 us  [shards(): key = add_one(lax.all_gather(w_key, 'seq', axis=0, tiled=True))]
    dynamic_update_slice x0 -> x16, local copies, waits for them, and re-layouts: none -> 12.1 us  [the longest x8 6.08 us: collect(): lax.dynamic_update_slice_in_dim(full, going_up, (here - far) % ways * lap...]
  transfers between devices with their start and end apart: 10 -> 24, of which waited for: 8 -> 14; matrix products, arithmetic and copies ran while one was open for 18% -> 25% of each run, Pallas kernels for 0% -> 0%
where the time goes in v1:
time: 415 us; the launch traced here: 414 us
  waiting for transfers between devices  235 us (57%)
  matrix products  78.2 us (19%)
  starting transfers between devices  51.6 us (12%)
  other arithmetic  18.4 us (4%)
  local copies, waits for them, and re-layouts  17.1 us (4%)
  between operations  13.7 us (3%)
    reduce_scatter x1, waiting for transfers between devices, shards(): lax.psum_scatter(terms.astype(jnp.bfloat16), 'hid', scatter_dimension=1,...  57.3 us
    all_gather x1, waiting for transfers between devices, shards(): query = add_one(lax.all_gather(w_query, 'seq', axis=0, tiled=True))  54.9 us
    ppermute x7, starting transfers between devices, collect(): lax.ppermute(going_down, axis, [(d, (d - 1) % ways) for d in range(ways)])  34.9 us
    all_gather x1, waiting for transfers between devices, shards(): key = add_one(lax.all_gather(w_key, 'seq', axis=0, tiled=True))  33.9 us
    ppermute x8, waiting for transfers between devices, collect(): lax.ppermute(going_up, axis, [(d, (d + 1) % ways) for d in range(ways)])  28.4 us
    ppermute x4, waiting for transfers between devices, shifted(): return lax.ppermute(x, axis, pairs)  27 us
    dot_general x3, matrix products, add_rows(): return jnp.dot(normed, piece, preferred_element_type=jnp.float32)  26.1 us
    sub x4, matrix products, one_head(): probs = jax.nn.softmax(scores, axis=-1).astype(jnp.bfloat16)  23.4 us
  transfers between devices with their start and end apart: 24, of which 14 were waited for; matrix products, arithmetic and copies ran while one was open for 25% of the time, Pallas kernels for 0%

profile of v1, /device:TPU:1, one launch (start us, length us, event | category | flops | bytes accessed | tf_op | source)
XLA Modules:
  0.0 414.5 jit_solution(12328304477273658841)
XLA Ops:
  11.5 4.8 %collective-permute-start.1 = (bf16[336,512]{1,0:T(8,128)(2,1)}, bf16[336,512]{1,0:T(8,128)(2,1)S(1)}, u32[]{:S(2)}, u32[]{:S(2)}) collective-permute-start(bf16[336,512]{1,0:T(8,128)(2,1)} %param.14), channel_id=1, source_target_pairs={{0,120},{8,0},{16,8},{24,16},{32,24},{40,32},{48,40},{56,48},{64,5... | collective-permute-start | bytes 1032200 | tf_op jit(solution)/shard_map/ppermute | solution.py:23
  16.3 7.9 %collective-permute-done = bf16[336,512]{1,0:T(8,128)(2,1)S(1)} collective-permute-done((bf16[336,512]{1,0:T(8,128)(2,1)}, bf16[336,512]{1,0:T(8,128)(2,1)S(1)}, u32[]{:S(2)}, u32[]{:S(2)}) %collective-permute-start) | collective-permute-done | bytes 344096 | tf_op jit(solution)/shard_map/ppermute | solution.py:20
  24.2 4.8 %collective-permute-start.3 = (bf16[336,512]{1,0:T(8,128)(2,1)S(1)}, bf16[336,512]{1,0:T(8,128)(2,1)S(1)}, u32[]{:S(2)}, u32[]{:S(2)}) collective-permute-start(bf16[336,512]{1,0:T(8,128)(2,1)S(1)} %collective-permute-done.1), channel_id=1, source_target_pairs={{0,120},{8,0},{16,8},{24,16},{32,24},{40,32},{48,40},{56,48},{64,5... | collective-permute-start | bytes 1032200 | tf_op jit(solution)/shard_map/ppermute | solution.py:23
  29.0 6.9 %collective-permute-done.2 = bf16[336,512]{1,0:T(8,128)(2,1)S(1)} collective-permute-done((bf16[336,512]{1,0:T(8,128)(2,1)S(1)}, bf16[336,512]{1,0:T(8,128)(2,1)S(1)}, u32[]{:S(2)}, u32[]{:S(2)}) %collective-permute-start.2) | collective-permute-done | bytes 344096 | tf_op jit(solution)/shard_map/ppermute | solution.py:20
  35.9 4.8 %collective-permute-start.5 = (bf16[336,512]{1,0:T(8,128)(2,1)S(1)}, bf16[336,512]{1,0:T(8,128)(2,1)S(1)}, u32[]{:S(2)}, u32[]{:S(2)}) collective-permute-start(bf16[336,512]{1,0:T(8,128)(2,1)S(1)} %collective-permute-done.3), channel_id=1, source_target_pairs={{0,120},{8,0},{16,8},{24,16},{32,24},{40,32},{48,40},{56,48},{64,5... | collective-permute-start | bytes 1032200 | tf_op jit(solution)/shard_map/ppermute | solution.py:23
  42.0 4.6 %collective-permute-done.4 = bf16[336,512]{1,0:T(8,128)(2,1)S(1)} collective-permute-done((bf16[336,512]{1,0:T(8,128)(2,1)S(1)}, bf16[336,512]{1,0:T(8,128)(2,1)S(1)}, u32[]{:S(2)}, u32[]{:S(2)}) %collective-permute-start.4) | collective-permute-done | bytes 344096 | tf_op jit(solution)/shard_map/ppermute | solution.py:20
  50.9 4.8 %collective-permute-start.7 = (bf16[336,512]{1,0:T(8,128)(2,1)S(1)}, bf16[336,512]{1,0:T(8,128)(2,1)S(1)}, u32[]{:S(2)}, u32[]{:S(2)}) collective-permute-start(bf16[336,512]{1,0:T(8,128)(2,1)S(1)} %collective-permute-done.5), channel_id=1, source_target_pairs={{0,120},{8,0},{16,8},{24,16},{32,24},{40,32},{48,40},{56,48},{64,5... | collective-permute-start | bytes 1032200 | tf_op jit(solution)/shard_map/ppermute | solution.py:23
  59.9 5.2 %collective-permute-start.9 = (bf16[336,512]{1,0:T(8,128)(2,1)S(1)}, bf16[336,512]{1,0:T(8,128)(2,1)S(1)}, u32[]{:S(2)}, u32[]{:S(2)}) collective-permute-start(bf16[336,512]{1,0:T(8,128)(2,1)S(1)} %collective-permute-done.7), channel_id=1, source_target_pairs={{0,120},{8,0},{16,8},{24,16},{32,24},{40,32},{48,40},{56,48},{64,5... | collective-permute-start | bytes 1032200 | tf_op jit(solution)/shard_map/ppermute | solution.py:23
  69.3 5.2 %collective-permute-start.11 = (bf16[336,512]{1,0:T(8,128)(2,1)S(1)}, bf16[336,512]{1,0:T(8,128)(2,1)S(1)}, u32[]{:S(2)}, u32[]{:S(2)}) collective-permute-start(bf16[336,512]{1,0:T(8,128)(2,1)S(1)} %collective-permute-done.9), channel_id=1, source_target_pairs={{0,120},{8,0},{16,8},{24,16},{32,24},{40,32},{48,40},{56,48},{64,5... | collective-permute-start | bytes 1032200 | tf_op jit(solution)/shard_map/ppermute | solution.py:23
  78.8 5.2 %collective-permute-start.13 = (bf16[336,512]{1,0:T(8,128)(2,1)S(1)}, bf16[336,512]{1,0:T(8,128)(2,1)S(1)}, u32[]{:S(2)}, u32[]{:S(2)}) collective-permute-start(bf16[336,512]{1,0:T(8,128)(2,1)S(1)} %collective-permute-done.11), channel_id=1, source_target_pairs={{0,120},{8,0},{16,8},{24,16},{32,24},{40,32},{48,40},{56,48},{64,5... | collective-permute-start | bytes 1032200 | tf_op jit(solution)/shard_map/ppermute | solution.py:23
  86.3 4.4 %collective-permute-done.13 = bf16[336,512]{1,0:T(8,128)(2,1)S(1)} collective-permute-done((bf16[336,512]{1,0:T(8,128)(2,1)S(1)}, bf16[336,512]{1,0:T(8,128)(2,1)S(1)}, u32[]{:S(2)}, u32[]{:S(2)}) %collective-permute-start.13) | collective-permute-done | bytes 344096 | tf_op jit(solution)/shard_map/ppermute | solution.py:23
  91.4 9.0 %collective-permute-done.14 = bf16[336,512]{1,0:T(8,128)(2,1)S(1)} collective-permute-done((bf16[336,512]{1,0:T(8,128)(2,1)S(1)}, bf16[336,512]{1,0:T(8,128)(2,1)S(1)}, u32[]{:S(2)}, u32[]{:S(2)}) %collective-permute-start.14) | collective-permute-done | bytes 344096 | tf_op jit(solution)/shard_map/ppermute | solution.py:20
  105.3 6.8 %convolution_convert_fusion.1 = bf16[512,512]{0,1:T(8,128)(2,1)} fusion(bf16[5376,512]{1,0:T(8,128)(2,1)} %constant_dynamic-update-slice_fusion, bf16[512,5376]{0,1:T(8,128)(2,1)S(1)} %copy-done, f32[5376]{0:T(1024)S(1)} %copy-done.4, f32[512]{0:T(512)S(1)} %add_rsqrt_fusion.2), kind=kOutput, calls=%fused_computation.47 | convolution fusion | flops 2829844480 | bytes 11557888 | tf_op jit(solution)/shard_map/dot_general | solution.py:54
  116.5 33.9 %all-gather.7.cloned.1.call-done = bf16[5376,512]{1,0:T(8,128)(2,1)} async-done(((bf16[336,512]{1,0:T(8,128)(2,1)}), bf16[5376,512]{1,0:T(8,128)(2,1)}) %all-gather.7.cloned.1.call-update) | async-done | bytes 5505040 | tf_op jit(solution)/shard_map/all_gather | solution.py:69
  150.4 7.6 %multiply_reduce_fusion.1 = (f32[512,4]{0,1:T(4,128)S(1)}, f32[512,512]{0,1:T(8,128)S(1)}) fusion(bf16[5376,512]{1,0:T(8,128)(2,1)} %all-gather.7.cloned.1.call-done, bf16[512,5376]{0,1:T(8,128)(2,1)} %all-gather.5.cloned.1.call-done, f32[5376]{0:T(1024)S(1)} %copy-done.4, f32[512]{0:T(512)S(1)} %add_rsqrt_fusion.2), kind=kOutput, calls=%fused_computation.52 | convolution fusion | flops 2830104576 | bytes 12090368 | tf_op jit(solution)/shard_map/dot_general | solution.py:54
  159.4 8.6 %collective-permute-start.17 = (bf16[512,4,128]{2,0,1:T(8,128)(2,1)S(1)}, bf16[512,4,128]{2,0,1:T(8,128)(2,1)S(1)}, u32[]{:S(2)}, u32[]{:S(2)}) collective-permute-start(bf16[512,4,128]{2,0,1:T(8,128)(2,1)S(1)} %pad_maximum_fusion), channel_id=1, source_target_pairs={{0,16},{8,24},{16,32},{24,40},{32,48},{40,56},{48,64},{56,72},{64,... | collective-permute-start | bytes 1572872 | tf_op jit(solution)/shard_map/ppermute | solution.py:33
  172.2 10.9 %collective-permute-done.17 = bf16[512,4,128]{2,0,1:T(8,128)(2,1)S(1)} collective-permute-done((bf16[512,4,128]{2,0,1:T(8,128)(2,1)S(1)}, bf16[512,4,128]{2,0,1:T(8,128)(2,1)S(1)}, u32[]{:S(2)}, u32[]{:S(2)}) %collective-permute-start.17) | collective-permute-done | bytes 524320 | tf_op jit(solution)/shard_map/ppermute | solution.py:33
  183.1 16.1 %collective-permute-done.18 = bf16[512,4,128]{2,0,1:T(8,128)(2,1)S(1)} collective-permute-done((bf16[512,4,128]{2,0,1:T(8,128)(2,1)S(1)}, bf16[512,4,128]{2,0,1:T(8,128)(2,1)S(1)}, u32[]{:S(2)}, u32[]{:S(2)}) %collective-permute-start.18) | collective-permute-done | bytes 524320 | tf_op jit(solution)/shard_map/ppermute | solution.py:33
  200.8 54.9 %all-gather.9.cloned.1.call-done = bf16[5376,1024]{1,0:T(8,128)(2,1)} async-done(((bf16[336,1024]{1,0:T(8,128)(2,1)}), bf16[5376,1024]{1,0:T(8,128)(2,1)}) %all-gather.9.cloned.1.call-update) | async-done | bytes 11010064 | tf_op jit(solution)/shard_map/all_gather | solution.py:68
  255.7 11.7 %convolution_bitcast_fusion = f32[64,8,8,128]{3,1,2,0:T(8,128)S(1)} fusion(bf16[5376,1024]{1,0:T(8,128)(2,1)} %all-gather.9.cloned.1.call-done, bf16[512,5376]{0,1:T(8,128)(2,1)} %all-gather.5.cloned.1.call-done, f32[5376]{0:T(1024)S(1)} %copy-done.4, f32[512]{0:T(512)S(1)} %add_rsqrt_fusion.2), kind=kOutput, calls=%fused_computation.44 | convolution fusion | flops 5648154624 | bytes 18635776 | tf_op jit(solution)/shard_map/dot_general | solution.py:54
  272.5 46.5 %while.11 = (s32[]{:T(128)}, bf16[4,512,2,128]{1,3,2,0:T(8,128)(2,1)}, bf16[4,1536,128]{1,2,0:T(8,128)(2,1)}, bf16[4,1536,128]{2,1,0:T(8,128)(2,1)}, bf16[4,512,...) while((s32[]{:T(128)}, ...), condition=%wide.region_6.7_spmd.clone, body=%wide.region_3.6_spmd.clone.sunk | while | flops 817235456 | bytes 15486557 | solution.py:107
  273.7 5.8 %fusion.75 = (f32[2,512]{1,0:T(2,128)S(1)}, f32[2,512,1536]{1,2,0:T(8,128)}) fusion(pred[512,1536]{0,1:T(8,128)(4,1)S(1)} %fusion.74, bf16[4,1536,128]{2,1,0:T(8,128)(2,1)} %get-tuple-element.159, s32[]{:T(128)} %get-tuple-element.147, bf16[4,512,2,128]{3,1,2,0:T(8,128)(2,1)S(1)} %get-tuple-element.160), kind=kOutput, calls=%fused_computation.81.clone.1 | convolution fusion | flops 407373312 | bytes 7738368 | tf_op jit(solution)/shard_map/while/body/eval_jaxpr/sub | solution.py:103
  279.6 4.3 %fusion.76 = bf16[4,512,2,128]{1,3,2,0:T(8,128)(2,1)} fusion(bf16[4,512,2,128]{1,3,2,0:T(8,128)(2,1)} %get-tuple-element.148, s32[]{:T(128)} %get-tuple-element.147, f32[2,512,1536]{1,2,0:T(8,128)} %get-tuple-element.136, f32[2,512]{1,0:T(2,128)S(1)} %get-tuple-element.137, bf16[4,1536,128]{1,2,0:T(8,128)(2,1)} %get-tuple-element.158), kind=kOutput, calls=%fused_computation.15.clone.1 | convolution fusion | flops 405929984 | bytes 6951936 | tf_op jit(solution)/shard_map/while/body/eval_jaxpr/grl,ld->rgd/dot_general | solution.py:104
  285.1 5.8 %fusion.75 = (f32[2,512]{1,0:T(2,128)S(1)}, f32[2,512,1536]{1,2,0:T(8,128)}) fusion(pred[512,1536]{0,1:T(8,128)(4,1)S(1)} %fusion.74, bf16[4,1536,128]{2,1,0:T(8,128)(2,1)} %get-tuple-element.159, s32[]{:T(128)} %get-tuple-element.147, bf16[4,512,2,128]{3,1,2,0:T(8,128)(2,1)S(1)} %get-tuple-element.160), kind=kOutput, calls=%fused_computation.81.clone.1 | convolution fusion | flops 407373312 | bytes 7738368 | tf_op jit(solution)/shard_map/while/body/eval_jaxpr/sub | solution.py:103
  290.9 5.1 %fusion.76 = bf16[4,512,2,128]{1,3,2,0:T(8,128)(2,1)} fusion(bf16[4,512,2,128]{1,3,2,0:T(8,128)(2,1)} %get-tuple-element.148, s32[]{:T(128)} %get-tuple-element.147, f32[2,512,1536]{1,2,0:T(8,128)} %get-tuple-element.136, f32[2,512]{1,0:T(2,128)S(1)} %get-tuple-element.137, bf16[4,1536,128]{1,2,0:T(8,128)(2,1)} %get-tuple-element.158), kind=kOutput, calls=%fused_computation.15.clone.1 | convolution fusion | flops 405929984 | bytes 6951936 | tf_op jit(solution)/shard_map/while/body/eval_jaxpr/grl,ld->rgd/dot_general | solution.py:104
  297.2 5.8 %fusion.75 = (f32[2,512]{1,0:T(2,128)S(1)}, f32[2,512,1536]{1,2,0:T(8,128)}) fusion(pred[512,1536]{0,1:T(8,128)(4,1)S(1)} %fusion.74, bf16[4,1536,128]{2,1,0:T(8,128)(2,1)} %get-tuple-element.159, s32[]{:T(128)} %get-tuple-element.147, bf16[4,512,2,128]{3,1,2,0:T(8,128)(2,1)S(1)} %get-tuple-element.160), kind=kOutput, calls=%fused_computation.81.clone.1 | convolution fusion | flops 407373312 | bytes 7738368 | tf_op jit(solution)/shard_map/while/body/eval_jaxpr/sub | solution.py:103
  303.1 4.5 %fusion.76 = bf16[4,512,2,128]{1,3,2,0:T(8,128)(2,1)} fusion(bf16[4,512,2,128]{1,3,2,0:T(8,128)(2,1)} %get-tuple-element.148, s32[]{:T(128)} %get-tuple-element.147, f32[2,512,1536]{1,2,0:T(8,128)} %get-tuple-element.136, f32[2,512]{1,0:T(2,128)S(1)} %get-tuple-element.137, bf16[4,1536,128]{1,2,0:T(8,128)(2,1)} %get-tuple-element.158), kind=kOutput, calls=%fused_computation.15.clone.1 | convolution fusion | flops 405929984 | bytes 6951936 | tf_op jit(solution)/shard_map/while/body/eval_jaxpr/grl,ld->rgd/dot_general | solution.py:104
  308.7 5.8 %fusion.75 = (f32[2,512]{1,0:T(2,128)S(1)}, f32[2,512,1536]{1,2,0:T(8,128)}) fusion(pred[512,1536]{0,1:T(8,128)(4,1)S(1)} %fusion.74, bf16[4,1536,128]{2,1,0:T(8,128)(2,1)} %get-tuple-element.159, s32[]{:T(128)} %get-tuple-element.147, bf16[4,512,2,128]{3,1,2,0:T(8,128)(2,1)S(1)} %get-tuple-element.160), kind=kOutput, calls=%fused_computation.81.clone.1 | convolution fusion | flops 407373312 | bytes 7738368 | tf_op jit(solution)/shard_map/while/body/eval_jaxpr/sub | solution.py:103
  314.6 4.4 %fusion.76 = bf16[4,512,2,128]{1,3,2,0:T(8,128)(2,1)} fusion(bf16[4,512,2,128]{1,3,2,0:T(8,128)(2,1)} %get-tuple-element.148, s32[]{:T(128)} %get-tuple-element.147, f32[2,512,1536]{1,2,0:T(8,128)} %get-tuple-element.136, f32[2,512]{1,0:T(2,128)S(1)} %get-tuple-element.137, bf16[4,1536,128]{1,2,0:T(8,128)(2,1)} %get-tuple-element.158), kind=kOutput, calls=%fused_computation.15.clone.1 | convolution fusion | flops 405929984 | bytes 6951936 | tf_op jit(solution)/shard_map/while/body/eval_jaxpr/grl,ld->rgd/dot_general | solution.py:104
  319.0 21.2 %all-gather.11.cloned.1.call-done = bf16[1024,5376]{0,1:T(8,128)(2,1)} async-done(((bf16[1024,336]{0,1:T(8,128)(2,1)}), bf16[1024,5376]{0,1:T(8,128)(2,1)}) %all-gather.11.cloned.1.call-update) | async-done | bytes 11010064 | tf_op jit(solution)/shard_map/all_gather | solution.py:111
  340.2 10.4 %convolution_convert_fusion = bf16[512,5376]{0,1:T(8,128)(2,1)} fusion(bf16[1024,5376]{0,1:T(8,128)(2,1)} %all-gather.11.cloned.1.call-done, bf16[512,1024]{0,1:T(8,128)(2,1)} %bitcast.83), kind=kOutput, calls=%fused_computation.37 | convolution fusion | flops 5639897088 | bytes 17563648 | tf_op jit(solution)/shard_map/dot_general | solution.py:109
  350.6 57.3 %reduce-scatter.2.cloned.1.call-done = bf16[512,1344]{0,1:T(8,128)(2,1)} async-done(((bf16[512,5376]{0,1:T(8,128)(2,1)}), bf16[512,1344]{0,1:T(8,128)(2,1)}) %reduce-scatter.2.cloned.1.call-update) | async-done | bytes 1376272 | tf_op jit(solution)/shard_map/reduce_scatter | solution.py:114
  (91 shorter events, 52.0 us)
Async XLA Ops:
  6.5 42.9 %copy-start.1 = (bf16[336,512]{1,0:T(8,128)(2,1)S(1)}, bf16[336,512]{1,0:T(8,128)(2,1)}, u32[]{:S(2)}) copy-start(bf16[336,512]{1,0:T(8,128)(2,1)} %param.14) | copy-start | bytes 1032196
  6.5 94.6 %all-gather.5.cloned.1.call-start = ((), (), s32[]{:S(2)}) async-start(), calls=%async_computation.1 | async-start | bytes 6881280 | tf_op jit(solution)/shard_map/all_gather | solution.py:58
  7.3 143.1 %all-gather.7.cloned.1.call-start = ((), (), s32[]{:S(2)}) async-start(), calls=%async_computation.2 | async-start | bytes 5849088 | tf_op jit(solution)/shard_map/all_gather | solution.py:69
  8.0 247.7 %all-gather.9.cloned.1.call-start = ((), (), s32[]{:S(2)}) async-start(), calls=%async_computation.3 | async-start | bytes 11698176 | tf_op jit(solution)/shard_map/all_gather | solution.py:68
  8.7 331.5 %all-gather.11.cloned.1.call-start = ((), (), s32[]{:S(2)}) async-start(), calls=%async_computation.4 | async-start | bytes 11698176 | tf_op jit(solution)/shard_map/all_gather | solution.py:111
  9.3 398.6 %reduce-scatter.2.cloned.1.call-start = ((), (), s32[]{:S(2)}) async-start(), calls=%async_computation.5 | async-start | bytes 6881280 | tf_op jit(solution)/shard_map/reduce_scatter | solution.py:114
  9.4 14.8 %collective-permute-start = (bf16[336,512]{1,0:T(8,128)(2,1)}, bf16[336,512]{1,0:T(8,128)(2,1)S(1)}, u32[]{:S(2)}, u32[]{:S(2)}) collective-permute-start(bf16[336,512]{1,0:T(8,128)(2,1)} %param.14), channel_id=1, source_target_pairs={{0,8},{8,16},{16,24},{24,32},{32,40},{40,48},{48,56},{56,64},{64,7... | collective-permute-start | bytes 1032200 | tf_op jit(solution)/shard_map/ppermute | solution.py:20
  11.5 12.7 %collective-permute-start.1 = (bf16[336,512]{1,0:T(8,128)(2,1)}, bf16[336,512]{1,0:T(8,128)(2,1)S(1)}, u32[]{:S(2)}, u32[]{:S(2)}) collective-permute-start(bf16[336,512]{1,0:T(8,128)(2,1)} %param.14), channel_id=1, source_target_pairs={{0,120},{8,0},{16,8},{24,16},{32,24},{40,32},{48,40},{56,48},{64,5... | collective-permute-start | bytes 1032200 | tf_op jit(solution)/shard_map/ppermute | solution.py:23
  24.2 11.6 %collective-permute-start.2 = (bf16[336,512]{1,0:T(8,128)(2,1)S(1)}, bf16[336,512]{1,0:T(8,128)(2,1)S(1)}, u32[]{:S(2)}, u32[]{:S(2)}) collective-permute-start(bf16[336,512]{1,0:T(8,128)(2,1)S(1)} %collective-permute-done), channel_id=1, source_target_pairs={{0,8},{8,16},{16,24},{24,32},{32,40},{40,48},{48,56},{56,64},{64,7... | collective-permute-start | bytes 1032200 | tf_op jit(solution)/shard_map/ppermute | solution.py:20
  24.2 11.7 %collective-permute-start.3 = (bf16[336,512]{1,0:T(8,128)(2,1)S(1)}, bf16[336,512]{1,0:T(8,128)(2,1)S(1)}, u32[]{:S(2)}, u32[]{:S(2)}) collective-permute-start(bf16[336,512]{1,0:T(8,128)(2,1)S(1)} %collective-permute-done.1), channel_id=1, source_target_pairs={{0,120},{8,0},{16,8},{24,16},{32,24},{40,32},{48,40},{56,48},{64,5... | collective-permute-start | bytes 1032200 | tf_op jit(solution)/shard_map/ppermute | solution.py:23
  35.9 10.7 %collective-permute-start.4 = (bf16[336,512]{1,0:T(8,128)(2,1)S(1)}, bf16[336,512]{1,0:T(8,128)(2,1)S(1)}, u32[]{:S(2)}, u32[]{:S(2)}) collective-permute-start(bf16[336,512]{1,0:T(8,128)(2,1)S(1)} %collective-permute-done.2), channel_id=1, source_target_pairs={{0,8},{8,16},{16,24},{24,32},{32,40},{40,48},{48,56},{56,64},{64,7... | collective-permute-start | bytes 1032200 | tf_op jit(solution)/shard_map/ppermute | solution.py:20
  35.9 15.1 %collective-permute-start.5 = (bf16[336,512]{1,0:T(8,128)(2,1)S(1)}, bf16[336,512]{1,0:T(8,128)(2,1)S(1)}, u32[]{:S(2)}, u32[]{:S(2)}) collective-permute-start(bf16[336,512]{1,0:T(8,128)(2,1)S(1)} %collective-permute-done.3), channel_id=1, source_target_pairs={{0,120},{8,0},{16,8},{24,16},{32,24},{40,32},{48,40},{56,48},{64,5... | collective-permute-start | bytes 1032200 | tf_op jit(solution)/shard_map/ppermute | solution.py:23
  46.6 9.9 %collective-permute-start.6 = (bf16[336,512]{1,0:T(8,128)(2,1)S(1)}, bf16[336,512]{1,0:T(8,128)(2,1)S(1)}, u32[]{:S(2)}, u32[]{:S(2)}) collective-permute-start(bf16[336,512]{1,0:T(8,128)(2,1)S(1)} %collective-permute-done.4), channel_id=1, source_target_pairs={{0,8},{8,16},{16,24},{24,32},{32,40},{40,48},{48,56},{56,64},{64,7... | collective-permute-start | bytes 1032200 | tf_op jit(solution)/shard_map/ppermute | solution.py:20
  50.9 9.0 %collective-permute-start.7 = (bf16[336,512]{1,0:T(8,128)(2,1)S(1)}, bf16[336,512]{1,0:T(8,128)(2,1)S(1)}, u32[]{:S(2)}, u32[]{:S(2)}) collective-permute-start(bf16[336,512]{1,0:T(8,128)(2,1)S(1)} %collective-permute-done.5), channel_id=1, source_target_pairs={{0,120},{8,0},{16,8},{24,16},{32,24},{40,32},{48,40},{56,48},{64,5... | collective-permute-start | bytes 1032200 | tf_op jit(solution)/shard_map/ppermute | solution.py:23
  56.5 9.4 %collective-permute-start.8 = (bf16[336,512]{1,0:T(8,128)(2,1)S(1)}, bf16[336,512]{1,0:T(8,128)(2,1)S(1)}, u32[]{:S(2)}, u32[]{:S(2)}) collective-permute-start(bf16[336,512]{1,0:T(8,128)(2,1)S(1)} %collective-permute-done.6), channel_id=1, source_target_pairs={{0,8},{8,16},{16,24},{24,32},{32,40},{40,48},{48,56},{56,64},{64,7... | collective-permute-start | bytes 1032200 | tf_op jit(solution)/shard_map/ppermute | solution.py:20
  59.9 9.4 %collective-permute-start.9 = (bf16[336,512]{1,0:T(8,128)(2,1)S(1)}, bf16[336,512]{1,0:T(8,128)(2,1)S(1)}, u32[]{:S(2)}, u32[]{:S(2)}) collective-permute-start(bf16[336,512]{1,0:T(8,128)(2,1)S(1)} %collective-permute-done.7), channel_id=1, source_target_pairs={{0,120},{8,0},{16,8},{24,16},{32,24},{40,32},{48,40},{56,48},{64,5... | collective-permute-start | bytes 1032200 | tf_op jit(solution)/shard_map/ppermute | solution.py:23
  65.9 9.4 %collective-permute-start.10 = (bf16[336,512]{1,0:T(8,128)(2,1)S(1)}, bf16[336,512]{1,0:T(8,128)(2,1)S(1)}, u32[]{:S(2)}, u32[]{:S(2)}) collective-permute-start(bf16[336,512]{1,0:T(8,128)(2,1)S(1)} %collective-permute-done.8), channel_id=1, source_target_pairs={{0,8},{8,16},{16,24},{24,32},{32,40},{40,48},{48,56},{56,64},{64,7... | collective-permute-start | bytes 1032200 | tf_op jit(solution)/shard_map/ppermute | solution.py:20
  67.4 37.6 %copy-start.4 = (f32[5376]{0:T(1024)S(1)}, f32[5376]{0:T(1024)}, u32[]{:S(2)}) copy-start(f32[5376]{0:T(1024)} %param.11) | copy-start | bytes 64516
  69.3 9.4 %collective-permute-start.11 = (bf16[336,512]{1,0:T(8,128)(2,1)S(1)}, bf16[336,512]{1,0:T(8,128)(2,1)S(1)}, u32[]{:S(2)}, u32[]{:S(2)}) collective-permute-start(bf16[336,512]{1,0:T(8,128)(2,1)S(1)} %collective-permute-done.9), channel_id=1, source_target_pairs={{0,120},{8,0},{16,8},{24,16},{32,24},{40,32},{48,40},{56,48},{64,5... | collective-permute-start | bytes 1032200 | tf_op jit(solution)/shard_map/ppermute | solution.py:23
  75.3 9.4 %collective-permute-start.12 = (bf16[336,512]{1,0:T(8,128)(2,1)S(1)}, bf16[336,512]{1,0:T(8,128)(2,1)S(1)}, u32[]{:S(2)}, u32[]{:S(2)}) collective-permute-start(bf16[336,512]{1,0:T(8,128)(2,1)S(1)} %collective-permute-done.10), channel_id=1, source_target_pairs={{0,8},{8,16},{16,24},{24,32},{32,40},{40,48},{48,56},{56,64},{64,7... | collective-permute-start | bytes 1032200 | tf_op jit(solution)/shard_map/ppermute | solution.py:20
  78.8 11.9 %collective-permute-start.13 = (bf16[336,512]{1,0:T(8,128)(2,1)S(1)}, bf16[336,512]{1,0:T(8,128)(2,1)S(1)}, u32[]{:S(2)}, u32[]{:S(2)}) collective-permute-start(bf16[336,512]{1,0:T(8,128)(2,1)S(1)} %collective-permute-done.11), channel_id=1, source_target_pairs={{0,120},{8,0},{16,8},{24,16},{32,24},{40,32},{48,40},{56,48},{64,5... | collective-permute-start | bytes 1032200 | tf_op jit(solution)/shard_map/ppermute | solution.py:23
  84.8 15.6 %collective-permute-start.14 = (bf16[336,512]{1,0:T(8,128)(2,1)S(1)}, bf16[336,512]{1,0:T(8,128)(2,1)S(1)}, u32[]{:S(2)}, u32[]{:S(2)}) collective-permute-start(bf16[336,512]{1,0:T(8,128)(2,1)S(1)} %collective-permute-done.12), channel_id=1, source_target_pairs={{0,8},{8,16},{16,24},{24,32},{32,40},{40,48},{48,56},{56,64},{64,7... | collective-permute-start | bytes 1032200 | tf_op jit(solution)/shard_map/ppermute | solution.py:20
  101.2 4.2 %copy-start = (bf16[512,5376]{0,1:T(8,128)(2,1)S(1)}, bf16[512,5376]{0,1:T(8,128)(2,1)}, u32[]{:S(2)}) copy-start(bf16[512,5376]{0,1:T(8,128)(2,1)} %all-gather.5.cloned.1.call-done) | copy-start | bytes 16515076
  112.2 46.1 %copy-start.2 = (f32[128]{0:T(128)S(1)}, f32[128]{0:T(128)}, u32[]{:S(2)}) copy-start(f32[128]{0:T(128)} %param.16) | copy-start | bytes 1540
  112.2 57.4 %collective-permute-start.15 = (bf16[512,4,128]{0,2,1:T(8,128)(2,1)}, bf16[512,4,128]{0,2,1:T(8,128)(2,1)}, u32[]{:S(2)}, u32[]{:S(2)}) collective-permute-start(bf16[512,4,128]{0,2,1:T(8,128)(2,1)} %bitcast), channel_id=1, source_target_pairs={{0,16},{8,24},{16,32},{24,40},{32,48},{40,56},{48,64},{56,72},{64,... | collective-permute-start | bytes 1572872 | tf_op jit(solution)/shard_map/ppermute | solution.py:33
  114.4 55.2 %collective-permute-start.16 = (bf16[512,4,128]{0,2,1:T(8,128)(2,1)}, bf16[512,4,128]{0,2,1:T(8,128)(2,1)}, u32[]{:S(2)}, u32[]{:S(2)}) collective-permute-start(bf16[512,4,128]{0,2,1:T(8,128)(2,1)} %bitcast), channel_id=1, source_target_pairs={{0,8},{8,16},{16,24},{24,32},{32,40},{40,48},{48,56},{56,64},{64,7... | collective-permute-start | bytes 1572872 | tf_op jit(solution)/shard_map/ppermute | solution.py:33
  159.4 23.7 %collective-permute-start.17 = (bf16[512,4,128]{2,0,1:T(8,128)(2,1)S(1)}, bf16[512,4,128]{2,0,1:T(8,128)(2,1)S(1)}, u32[]{:S(2)}, u32[]{:S(2)}) collective-permute-start(bf16[512,4,128]{2,0,1:T(8,128)(2,1)S(1)} %pad_maximum_fusion), channel_id=1, source_target_pairs={{0,16},{8,24},{16,32},{24,40},{32,48},{40,56},{48,64},{56,72},{64,... | collective-permute-start | bytes 1572872 | tf_op jit(solution)/shard_map/ppermute | solution.py:33
  168.0 31.3 %collective-permute-start.18 = (bf16[512,4,128]{2,0,1:T(8,128)(2,1)S(1)}, bf16[512,4,128]{2,0,1:T(8,128)(2,1)S(1)}, u32[]{:S(2)}, u32[]{:S(2)}) collective-permute-start(bf16[512,4,128]{2,0,1:T(8,128)(2,1)S(1)} %pad_maximum_fusion), channel_id=1, source_target_pairs={{0,8},{8,16},{16,24},{24,32},{32,40},{40,48},{48,56},{56,64},{64,7... | collective-permute-start | bytes 1572872 | tf_op jit(solution)/shard_map/ppermute | solution.py:33
  267.4 1.4 copy-start.3
Sparse Core Ops, SparseCore 0:
  9.0 62.3 all-gather.4
  73.5 76.7 all-gather.6
  152.5 103.1 all-gather.8
  257.7 82.4 all-gather.10
  350.8 57.1 reduce-scatter.1
